TPU v7x, 512 devices: a whole 4x4x16 slice. The times are simulated.
512 devices in a mesh: gx: 32 (over z, core), gy: 16 (over y, x).
Axes of the slice: x: 4, y: 4, z: 16, core: 2. Of those that a mesh axis runs over, the one named last changes fastest.
Arguments:
- velocity: float32 [3, 6144, 8192], P(None, 'gx', 'gy'), may hold values from -6 to 6
- row_owner: int32 [32, 64], P('gx'), may hold values from 0 to 15, as said below
- cell_list: int32 [4, 262144], P(None, ('gx', 'gy')), may hold values from 0 to 786431
- weights: float32 [4, 262144], P(None, ('gx', 'gy')), may hold values from 0.05 to 0.5
- offsets: float32 [262144], P(('gx', 'gy')), may hold values from -0.5 to 0.5
- relax_rate: float32 [262144], P(('gx', 'gy')), may hold values from 0.05 to 0.8
- particle_velocity: float32 [3, 262144], P(None, ('gx', 'gy')), may hold values from -6 to 6
- live_counts: int32 [2048], P(('gx', 'gy')), may hold values from 1 to 128, as said below
Outputs:
- gradient: float32 [3, 6144, 8192], P(None, 'gx', 'gy')
- fluid_at_particle: float32 [3, 262144], P(None, ('gx', 'gy'))
- updated_velocity: float32 [3, 262144], P(None, ('gx', 'gy'))
Inputs may be any that keep to these rules, and one draw needn't show every extreme that they name: `row_owner`: for every gx index and every gy index, at most 2 of that device's 4 row blocks name one owner; in every row of devices along gy one owner is named by exactly 2 blocks of every device; every owner is named by some block of the row. `live_counts`: the live particles of a block are its first slots.
All inputs are finite; a program needn't handle non-finite values.
Results may differ from a plain program's by a relative error of at most 0.0029.
Values may be sent and summed in bfloat16 or wider, within the bound.
A program may use at most 128 MiB of HBM per device.

v0:
```python
import math
import jax
import jax.numpy as jnp
from jax import lax
from jax.sharding import PartitionSpec as P

ROWB = 128
PSIZE = 128
R_DECAY = (3.0 - math.sqrt(5.0)) / 2.0
A_COEF = 14.0 / 9.0
B_COEF = 1.0 / 9.0
PRECISION_HIGH = lax.Precision.HIGHEST


def extended(cells, sides, width):
    for axis, dim in sides:
        count = lax.axis_size(axis)
        head = lax.slice_in_dim(cells, 0, width, axis=dim)
        tail = lax.slice_in_dim(cells, cells.shape[dim] - width, cells.shape[dim], axis=dim)
        cells = jnp.concatenate(
            [
                lax.ppermute(tail, axis, [(i, (i + 1) % count) for i in range(count)]),
                cells,
                lax.ppermute(head, axis, [((i + 1) % count, i) for i in range(count)]),
            ],
            axis=dim,
        )
    return cells


def stencil_sum(values, weights, offsets):
    carried = values[:3].astype(jnp.float32)
    slopes = values[3:].astype(jnp.float32)
    return jnp.sum(weights[None] * (carried + offsets[None, None] * slopes), 1)


def pick_cells(table, row_ids, line_ids):
    row_width = table.shape[2]
    picked = jnp.take(table, row_ids.reshape(-1), axis=1)
    select = jnp.arange(row_width)[None, :] == line_ids.reshape(-1)[:, None]
    values = jnp.sum(jnp.where(select[None], picked, jnp.zeros((), table.dtype)), -1)
    return values.reshape((table.shape[0],) + row_ids.shape)


def signed_power(exponent):
    parity = 1.0 - 2.0 * (exponent % 2).astype(jnp.float32)
    return parity * R_DECAY ** exponent.astype(jnp.float32)


def triangle(x_cells, backward):
    position = jnp.arange(x_cells)
    distance = position[:, None] - position[None, :]
    if backward:
        distance = -distance
    return jnp.where(distance >= 0, signed_power(jnp.abs(distance)), 0.0)


def widened_solve(velocity):
    components, x_cells, local_lines = velocity.shape
    margin = 20
    extent = x_cells + 2 * margin
    padded = extended(velocity, (("gx", 1),), margin + 2)
    right_side = 0.5 * A_COEF * (
        padded[:, 3 : extent + 3] - padded[:, 1 : extent + 1]
    ) + 0.25 * B_COEF * (padded[:, 4 : extent + 4] - padded[:, 0:extent])
    forward = jnp.einsum(
        "ij,cjl->cil", triangle(extent, False), right_side, precision=PRECISION_HIGH
    )
    backward = jnp.einsum("ij,cjl->cil", triangle(extent, True), forward, precision=PRECISION_HIGH)
    return 3.0 * R_DECAY * backward[:, margin : margin + x_cells]


def per_device(
    velocity, row_owner, cell_list, weights, offsets, relax_rate, particle_velocity, live_counts
):
    components, x_cells, local_lines = velocity.shape
    gradient = widened_solve(velocity)
    fields = jnp.concatenate([velocity, gradient], 0).astype(jnp.bfloat16)
    my_owner = lax.axis_index("gy")
    owners = lax.axis_size("gy")
    block_total = local_lines // ROWB
    capacity = block_total // 2
    column = row_owner[0]
    x_index = cell_list % x_cells
    remainder = cell_list // x_cells
    line_index = remainder % ROWB
    slot_ids = remainder // ROWB
    own_routes = lax.dynamic_slice_in_dim(column, my_owner * block_total, block_total)
    ordinal = jnp.arange(block_total)
    earlier_same = (own_routes[:, None] == own_routes[None, :]) & (
        ordinal[None, :] < ordinal[:, None]
    )
    ranking = jnp.sum(earlier_same.astype(jnp.int32), 1)
    slot_index = own_routes * capacity + ranking
    matches = (slot_index[None, :] == jnp.arange(owners * capacity)[:, None]).astype(jnp.bfloat16)
    blocked = fields.reshape(6, x_cells, block_total, ROWB)
    outgoing = jnp.einsum("ckbr,sb->cksr", blocked, matches, preferred_element_type=jnp.bfloat16)
    outgoing = outgoing.reshape(6, x_cells, owners, capacity, ROWB)
    arrived = lax.all_to_all(outgoing, "gy", split_axis=2, concat_axis=2, tiled=True)
    table = arrived.reshape(6, x_cells * owners * capacity, ROWB)
    row_ids = x_index * (owners * capacity) + slot_ids
    raw = stencil_sum(pick_cells(table, row_ids, line_index), weights, offsets)
    particle_slots = weights.shape[1]
    alive = (jnp.arange(PSIZE)[None, :] < live_counts[:, None]).reshape(particle_slots)
    fluid_at_particle = jnp.where(alive[None], raw, 0.0)
    updated_velocity = jnp.where(
        alive[None],
        particle_velocity + relax_rate[None] * (fluid_at_particle - particle_velocity),
        particle_velocity,
    )
    return (gradient, fluid_at_particle, updated_velocity)


def solution(mesh):
    return jax.shard_map(
        per_device,
        mesh=mesh,
        in_specs=(
            P(None, "gx", "gy"),
            P("gx", None),
            P(None, ("gx", "gy")),
            P(None, ("gx", "gy")),
            P(("gx", "gy")),
            P(("gx", "gy")),
            P(None, ("gx", "gy")),
            P(("gx", "gy")),
        ),
        out_specs=(P(None, "gx", "gy"), P(None, ("gx", "gy")), P(None, ("gx", "gy"))),
        check_vma=False,
    )
```

profile of v0, /device:TPU:417, one launch (start us, length us, event | category | flops | bytes accessed | tf_op | source)
XLA Modules:
  0.0 247.8 jit_solution(14806160395370510572)
XLA Ops:
  0.6 0.0 copy-start.6
  0.6 1.0 fusion.99
  1.7 1.3 collective-permute-start
  3.0 0.0 collective-permute-start.1
  3.0 0.0 copy-start
  3.0 1.4 convert.11
  4.4 0.0 copy-done.6
  4.4 0.1 fusion.82
  4.5 0.2 convert_reduce_fusion
  4.7 0.1 concatenate.13
  4.8 0.1 fusion.79
  4.9 0.2 collective-permute-done
  5.1 2.5 collective-permute-done.1
  7.5 0.0 copy-done
  7.5 0.2 pad_maximum_fusion
  7.7 2.0 convolution_bitcast_fusion.1
  9.8 1.5 convolution_bitcast_fusion
  11.3 1.2 fusion.98
  12.6 0.1 concatenate.14
  12.7 3.1 %fusion.7 = bf16[32,6,192,128]{3,0,2,1:T(8,128)(2,1)S(1)} fusion(bf16[3,192,4,128]{3,2,1,0:T(4,128)(2,1)S(1)} %concatenate.14, bf16[3,192,4,128]{3,2,1,0:T(4,128)(2,1)S(1)} %concatenate.13, s32[4]{0:T(128)S(1)} %fusion.79), kind=kOutput, calls=%fused_computation.13 | convolution fusion | flops 40108160 | bytes 10616848 | tf_op jit(solution)/shard_map/ckbr,sb->cksr/dot_general | solution.py:97
  15.8 10.2 %copy.30 = bf16[6,192,16,2,128]{4,3,1,0,2:T(2,128)(2,1)} copy(bf16[6,192,16,2,128]{4,3,2,1,0:T(2,128)(2,1)S(1)} %bitcast.45) | data formatting | bytes 18874368 | tf_op jit(solution)/shard_map/reshape | solution.py:98
  26.0 0.0 copy-start.2
  26.0 0.0 copy-start.7
  26.0 6.9 %all-to-all-start = ((bf16[6,192,16,2,128]{4,3,1,0,2:T(2,128)(2,1)}), bf16[6,192,16,2,128]{4,3,1,0,2:T(2,128)(2,1)}, u32[]{:S(2)}, u32[]{:S(2)}) async-start(bf16[6,192,16,2,128]{4,3,1,0,2:T(2,128)(2,1)} %copy.30), calls=%async_computation | async-start | bytes 18874368 | tf_op jit(solution)/shard_map/all_to_all | solution.py:99
  33.0 0.0 copy-done.2
  33.1 0.0 copy-done.7
  33.1 0.1 fusion.74
  33.2 0.3 iota_compare_fusion
  33.5 144.0 %all-to-all-done = bf16[6,192,16,2,128]{4,3,1,0,2:T(2,128)(2,1)} async-done(((bf16[6,192,16,2,128]{4,3,1,0,2:T(2,128)(2,1)}), bf16[6,192,16,2,128]{4,3,1,0,2:T(2,128)(2,1)}, u32[]{:S(2)}, u32[]{:S(2)}) %all-to-all-start) | async-done | bytes 9437216 | tf_op jit(solution)/shard_map/all_to_all | solution.py:99
  177.6 19.0 %copy.31 = bf16[6,192,16,2,128]{4,0,3,2,1:T(8,128)(2,1)} copy(bf16[6,192,16,2,128]{4,3,1,0,2:T(2,128)(2,1)} %all-to-all-done) | data formatting | bytes 18874368 | tf_op jit(solution)/shard_map/all_to_all | solution.py:99
  196.6 19.3 %gather_fusion = bf16[2048,6,128]{2,1,0:T(8,128)(2,1)} fusion(bf16[6,6144,128]{2,0,1:T(8,128)(2,1)} %bitcast.46, s32[2048]{0:T(1024)S(1)} %broadcast_clamp_fusion), kind=kCustom, calls=%fused_computation | custom fusion | bytes 6299648 | tf_op jit(solution)/shard_map/jit(_take)/gather | solution.py:39
  215.9 30.1 %select_reduce_fusion = bf16[2048,6]{1,0:T(8,128)(2,1)S(1)} fusion(bf16[2048,6,128]{2,1,0:T(8,128)(2,1)} %gather_fusion, pred[2048]{0:T(1024)(128)(4,1)S(1)} %compare_and_fusion, pred[2048,128]{1,0:T(8,128)(4,1)S(1)} %iota_compare_fusion), kind=kLoop, calls=%fused_computation.1 | loop fusion | flops 4706304 | bytes 3434496 | tf_op jit(solution)/shard_map/reduce_sum | solution.py:41
  246.0 0.0 copy-start.1
  246.0 0.0 copy-start.4
  246.0 0.0 copy-start.3
  246.0 0.0 copy-start.5
  246.0 0.2 fusion.100
  246.2 0.4 copy-done.1
  246.7 0.0 copy-done.4
  246.7 0.4 fusion.13
  247.1 0.1 copy.32
  247.2 0.0 copy-done.3
  247.2 0.0 copy-done.5
  247.2 0.6 add_select_fusion.2
  (7 shorter events, 0.1 us)
Async XLA Ops:
  0.6 3.8 %copy-start.6 = (s32[1,64]{1,0:T(1,128)S(1)}, s32[1,64]{1,0:T(1,128)}, u32[]{:S(2)}) copy-start(s32[1,64]{1,0:T(1,128)} %param.9) | copy-start | bytes 772
  1.7 3.4 %collective-permute-start = (f32[3,22,512]{2,1,0:T(8,128)S(1)}, f32[3,22,512]{2,1,0:T(8,128)S(1)}, u32[]{:S(2)}, u32[]{:S(2)}) collective-permute-start(f32[3,22,512]{2,1,0:T(8,128)S(1)} %get-tuple-element.13), channel_id=1, source_target_pairs={{0,16},{16,32},{32,48},{48,64},{64,80},{80,96},{96,112},{112,128},... | collective-permute-start | bytes 405512 | tf_op jit(solution)/shard_map/ppermute | solution.py:22
  3.0 4.6 %collective-permute-start.1 = (f32[3,22,512]{2,1,0:T(8,128)S(1)}, f32[3,22,512]{2,1,0:T(8,128)S(1)}, u32[]{:S(2)}, u32[]{:S(2)}) collective-permute-start(f32[3,22,512]{2,1,0:T(8,128)S(1)} %get-tuple-element.14), channel_id=1, source_target_pairs={{16,0},{32,16},{48,32},{64,48},{80,64},{96,80},{112,96},{128,112},... | collective-permute-start | bytes 405512 | tf_op jit(solution)/shard_map/ppermute | solution.py:24
  3.0 4.6 %copy-start = (f32[3,192,512]{2,1,0:T(8,128)S(1)}, f32[3,192,512]{2,1,0:T(8,128)}, u32[]{:S(2)}) copy-start(f32[3,192,512]{2,1,0:T(8,128)} %param.8) | copy-start | bytes 3538948
  26.0 7.0 %copy-start.2 = (s32[4,512]{1,0:T(4,128)S(1)}, s32[4,512]{1,0:T(4,128)}, u32[]{:S(2)}) copy-start(s32[4,512]{1,0:T(4,128)} %param.10) | copy-start | bytes 24580
  26.0 7.0 %copy-start.7 = (s32[4]{0:T(128)S(1)}, s32[4]{0:T(128)}, u32[]{:S(2)}) copy-start(s32[4]{0:T(128)} %param.15) | copy-start | bytes 52
  26.0 151.5 %all-to-all-start = ((bf16[6,192,16,2,128]{4,3,1,0,2:T(2,128)(2,1)}), bf16[6,192,16,2,128]{4,3,1,0,2:T(2,128)(2,1)}, u32[]{:S(2)}, u32[]{:S(2)}) async-start(bf16[6,192,16,2,128]{4,3,1,0,2:T(2,128)(2,1)} %copy.30), calls=%async_computation | async-start | bytes 18874368 | tf_op jit(solution)/shard_map/all_to_all | solution.py:99
  246.0 0.7 copy-start.1
  246.0 0.7 copy-start.4
  246.0 1.2 copy-start.3
  246.0 1.2 copy-start.5
where the time goes:
time: 248 us
  waiting for transfers between devices  147 us (59%)
  local copies, waits for them, and re-layouts  50.7 us (20%)
  other arithmetic  34.7 us (14%)
  starting transfers between devices  8.25 us (3%)
  matrix products  6.66 us (3%)
    all_to_all x1, waiting for transfers between devices, per_device(): lax.all_to_all(outgoing, 'gy', split_axis=2, concat_axis=2, tiled=True)  144 us
    reduce_sum x1, other arithmetic, pick_cells(): jnp.sum(jnp.where(select[None], picked, jnp.zeros((), table.dtype)), -1)  30.1 us
    gather x1, local copies, waits for them, and re-layouts, pick_cells(): picked = jnp.take(table, row_ids.reshape(-1), axis=1)  19.3 us
    all_to_all x1, local copies, waits for them, and re-layouts, per_device(): lax.all_to_all(outgoing, 'gy', split_axis=2, concat_axis=2, tiled=True)  19 us
    reshape x1, local copies, waits for them, and re-layouts, per_device(): outgoing = outgoing.reshape(6, x_cells, owners, capacity, ROWB)  10.2 us
    all_to_all x1, starting transfers between devices, per_device(): lax.all_to_all(outgoing, 'gy', split_axis=2, concat_axis=2, tiled=True)  6.94 us
  transfers between devices with their start and end apart: 3, of which 3 were waited for; matrix products, arithmetic and copies ran while one was open for 1% of the time, Pallas kernels for 0%

commit v1 on v0

--- a/solution.py
+++ b/solution.py
@@ -96,7 +96,11 @@
     blocked = fields.reshape(6, x_cells, block_total, ROWB)
     outgoing = jnp.einsum("ckbr,sb->cksr", blocked, matches, preferred_element_type=jnp.bfloat16)
     outgoing = outgoing.reshape(6, x_cells, owners, capacity, ROWB)
-    arrived = lax.all_to_all(outgoing, "gy", split_axis=2, concat_axis=2, tiled=True)
+    carry_out = lax.axis_size("gy")
+    mixed_arr = jnp.split(outgoing, carry_out, axis=2)
+    parts_out = jnp.stack(mixed_arr)
+    top = lax.all_to_all(parts_out, "gy", 0, 0)
+    arrived = jnp.concatenate(top, axis=2)
     table = arrived.reshape(6, x_cells * owners * capacity, ROWB)
     row_ids = x_index * (owners * capacity) + slot_ids
     raw = stencil_sum(pick_cells(table, row_ids, line_index), weights, offsets)

time: 248 us -> 284 us (1.15)
  the two profiles are of different devices: /device:TPU:417 before, /device:TPU:193 now
where the time goes in v1:
time: 284 us
  waiting for transfers between devices  144 us (51%)
  local copies, waits for them, and re-layouts  86.7 us (31%)
  other arithmetic  36.5 us (13%)
  starting transfers between devices  9.15 us (3%)
  matrix products  6.85 us (2%)
    all_to_all x1, waiting for transfers between devices, per_device(): top = lax.all_to_all(parts_out, 'gy', 0, 0)  143 us
    another operation x1, local copies, waits for them, and re-layouts, per_device(): table = arrived.reshape(6, x_cells * owners * capacity, ROWB)  37 us
    reduce_sum x1, other arithmetic, pick_cells(): jnp.sum(jnp.where(select[None], picked, jnp.zeros((), table.dtype)), -1)  30.1 us
    gather x1, local copies, waits for them, and re-layouts, pick_cells(): picked = jnp.take(table, row_ids.reshape(-1), axis=1)  19.4 us
    unnamed x30, local copies, waits for them, and re-layouts  18.6 us
    reshape x1, local copies, waits for them, and re-layouts, per_device(): arrived = jnp.concatenate(top, axis=2)  8.15 us
    all_to_all x1, starting transfers between devices, per_device(): top = lax.all_to_all(parts_out, 'gy', 0, 0)  6.94 us
  transfers between devices with their start and end apart: 3, of which 2 were waited for; matrix products, arithmetic and copies ran while one was open for 1% of the time, Pallas kernels for 0%

profile of v1, /device:TPU:193, one launch (start us, length us, event | category | flops | bytes accessed | tf_op | source)
XLA Modules:
  0.0 284.1 jit_solution(437558069760138243)
XLA Ops:
  0.6 1.0 fusion.115
  1.6 2.2 collective-permute-start
  3.9 0.0 collective-permute-start.1
  3.9 1.3 convert.11
  5.2 0.7 fusion.98
  5.9 0.2 convert_reduce_fusion
  6.1 0.1 concatenate.13
  6.3 0.7 fusion.95
  7.0 0.0 collective-permute-done
  7.0 1.4 collective-permute-done.1
  8.4 1.4 pad_maximum_fusion
  9.9 2.0 convolution_bitcast_fusion.1
  11.9 1.5 convolution_bitcast_fusion
  13.5 1.2 fusion.114
  14.7 0.1 concatenate.14
  14.9 3.3 %fusion.7 = bf16[32,6,192,128]{3,0,2,1:T(8,128)(2,1)S(1)} fusion(bf16[3,192,4,128]{3,2,1,0:T(4,128)(2,1)S(1)} %concatenate.14, bf16[3,192,4,128]{3,2,1,0:T(4,128)(2,1)S(1)} %concatenate.13, s32[4]{0:T(128)S(1)} %fusion.95), kind=kOutput, calls=%fused_computation.13 | convolution fusion | flops 40108160 | bytes 10616848 | tf_op jit(solution)/shard_map/ckbr,sb->cksr/dot_general | solution.py:97
  18.1 1.2 fusion.31
  19.4 1.2 fusion.30
  20.6 1.2 fusion.29
  21.8 1.2 fusion.28
  23.0 1.2 fusion.27
  24.3 1.3 fusion.26
  25.5 1.3 fusion.25
  26.8 1.2 fusion.24
  28.0 1.2 fusion.23
  29.3 1.2 fusion.22
  30.5 1.3 fusion.21
  31.7 1.2 fusion.20
  33.0 1.2 fusion.19
  34.2 1.3 fusion.18
  35.4 1.2 fusion.17
  36.7 1.2 fusion.16
  37.9 0.0 copy-start.1
  37.9 0.0 copy-start.5
  37.9 6.9 %all-to-all-start = ((bf16[16,6,192,1,2,128]{5,4,2,1,3,0:T(2,128)(2,1)}), bf16[16,6,192,1,2,128]{5,4,2,1,3,0:T(2,128)(2,1)}, u32[]{:S(2)}, u32[]{:S(2)}) async-start(bf16[16,6,192,1,2,128]{5,4,2,1,3,0:T(2,128)(2,1)} %fusion.16), calls=%async_computation | async-start | bytes 18874368 | tf_op jit(solution)/shard_map/all_to_all | solution.py:102
  44.9 0.0 copy-done.1
  45.0 0.0 copy-done.5
  45.0 0.1 fusion.90
  45.1 0.3 iota_compare_fusion
  45.4 142.6 %all-to-all-done = bf16[16,6,192,1,2,128]{5,4,2,1,3,0:T(2,128)(2,1)} async-done(((bf16[16,6,192,1,2,128]{5,4,2,1,3,0:T(2,128)(2,1)}), bf16[16,6,192,1,2,128]{5,4,2,1,3,0:T(2,128)(2,1)}, u32[]{:S(2)}, u32[]{:S(2)}) %all-to-all-start) | async-done | bytes 9437216 | tf_op jit(solution)/shard_map/all_to_all | solution.py:102
  188.1 8.1 %copy.125 = bf16[6,192,16,1,2,128]{5,4,2,1,0,3:T(2,128)(2,1)S(1)} copy(bf16[6,192,16,1,2,128]{5,4,1,0,3,2:T(2,128)(2,1)} %bitcast.29) | data formatting | bytes 18874368 | tf_op jit(solution)/shard_map/reshape | solution.py:103
  196.2 37.0 %copy.126 = bf16[6,6144,128]{2,0,1:T(8,128)(2,1)} copy(bf16[6,6144,128]{2,1,0:T(8,128)(2,1)S(1)} %bitcast.158) | data formatting | bytes 18874368 | tf_op jit(solution)/shard_map/reshape;reshape | solution.py:104
  233.3 0.0 copy-start
  233.3 0.0 copy-start.3
  233.3 0.0 copy-start.2
  233.3 0.0 copy-start.4
  233.3 19.4 %gather_fusion = bf16[2048,6,128]{2,1,0:T(8,128)(2,1)} fusion(bf16[6,6144,128]{2,0,1:T(8,128)(2,1)} %copy.126, s32[2048]{0:T(1024)S(1)} %broadcast_clamp_fusion), kind=kCustom, calls=%fused_computation | custom fusion | bytes 6299648 | tf_op jit(solution)/shard_map/jit(_take)/gather | solution.py:39
  252.6 30.1 %select_reduce_fusion = bf16[2048,6]{1,0:T(8,128)(2,1)S(1)} fusion(bf16[2048,6,128]{2,1,0:T(8,128)(2,1)} %gather_fusion, pred[2048]{0:T(1024)(128)(4,1)S(1)} %compare_and_fusion, pred[2048,128]{1,0:T(8,128)(4,1)S(1)} %iota_compare_fusion), kind=kLoop, calls=%fused_computation.1 | loop fusion | flops 4706304 | bytes 3434496 | tf_op jit(solution)/shard_map/reduce_sum | solution.py:41
  282.7 0.2 fusion.116
  282.9 0.0 copy-done
  282.9 0.0 copy-done.3
  282.9 0.4 fusion.13
  283.3 0.1 copy.127
  283.4 0.0 copy-done.2
  283.4 0.0 copy-done.4
  283.4 0.6 add_select_fusion.2
  (7 shorter events, 0.1 us)
Async XLA Ops:
  1.6 5.4 %collective-permute-start = (f32[3,22,512]{2,1,0:T(8,128)S(1)}, f32[3,22,512]{2,1,0:T(8,128)S(1)}, u32[]{:S(2)}, u32[]{:S(2)}) collective-permute-start(f32[3,22,512]{2,1,0:T(8,128)S(1)} %get-tuple-element.13), channel_id=1, source_target_pairs={{0,16},{16,32},{32,48},{48,64},{64,80},{80,96},{96,112},{112,128},... | collective-permute-start | bytes 405512 | tf_op jit(solution)/shard_map/ppermute | solution.py:22
  3.9 4.6 %collective-permute-start.1 = (f32[3,22,512]{2,1,0:T(8,128)S(1)}, f32[3,22,512]{2,1,0:T(8,128)S(1)}, u32[]{:S(2)}, u32[]{:S(2)}) collective-permute-start(f32[3,22,512]{2,1,0:T(8,128)S(1)} %get-tuple-element.14), channel_id=1, source_target_pairs={{16,0},{32,16},{48,32},{64,48},{80,64},{96,80},{112,96},{128,112},... | collective-permute-start | bytes 405512 | tf_op jit(solution)/shard_map/ppermute | solution.py:24
  37.9 7.0 %copy-start.1 = (s32[4,512]{1,0:T(4,128)S(1)}, s32[4,512]{1,0:T(4,128)}, u32[]{:S(2)}) copy-start(s32[4,512]{1,0:T(4,128)} %param.10) | copy-start | bytes 24580
  37.9 7.0 %copy-start.5 = (s32[4]{0:T(128)S(1)}, s32[4]{0:T(128)}, u32[]{:S(2)}) copy-start(s32[4]{0:T(128)} %param.15) | copy-start | bytes 52
  37.9 150.1 %all-to-all-start = ((bf16[16,6,192,1,2,128]{5,4,2,1,3,0:T(2,128)(2,1)}), bf16[16,6,192,1,2,128]{5,4,2,1,3,0:T(2,128)(2,1)}, u32[]{:S(2)}, u32[]{:S(2)}) async-start(bf16[16,6,192,1,2,128]{5,4,2,1,3,0:T(2,128)(2,1)} %fusion.16), calls=%async_computation | async-start | bytes 18874368 | tf_op jit(solution)/shard_map/all_to_all | solution.py:102
  233.3 49.6 %copy-start = (f32[4,512]{1,0:T(4,128)S(1)}, f32[4,512]{1,0:T(4,128)}, u32[]{:S(2)}) copy-start(f32[4,512]{1,0:T(4,128)} %param.11) | copy-start | bytes 24580
  233.3 49.6 %copy-start.3 = (f32[512]{0:T(512)S(1)}, f32[512]{0:T(512)}, u32[]{:S(2)}) copy-start(f32[512]{0:T(512)} %param.12) | copy-start | bytes 6148
  233.3 50.2 %copy-start.2 = (f32[3,512]{1,0:T(4,128)S(1)}, f32[3,512]{1,0:T(4,128)}, u32[]{:S(2)}) copy-start(f32[3,512]{1,0:T(4,128)} %param.14) | copy-start | bytes 18436
  233.3 50.2 %copy-start.4 = (f32[512]{0:T(512)S(1)}, f32[512]{0:T(512)}, u32[]{:S(2)}) copy-start(f32[512]{0:T(512)} %param.13) | copy-start | bytes 6148
